TPU v7x, 256 devices: a whole 4x4x8 slice. The times are simulated.
256 devices in a mesh: sec: 4 (over y_lo, core), mom: 8 (over x, y_hi), en: 8 (over z).
Axes of the slice: x: 4, y: 4 (y_hi: 2, y_lo: 2; y = y_hi * 2 + y_lo), z: 8, core: 2. Of those that a mesh axis runs over, the one named last changes fastest.
Arguments:
- green_blocks: bfloat16 [8, 64, 2, 128, 128], P('mom', ('sec', 'en')), may hold values from -6 to 6
- derivative: bfloat16 [3, 128, 128], replicated, may hold values from -0.5 to 0.5
- bare_phonon: float32 [4, 8, 2, 3, 3, 128], P('sec', 'mom'), may hold values from -4 to 4
- prior_polar: float32 [4, 8, 2, 3, 3, 128], P('sec', 'mom'), may hold values from -4 to 4
- offsets: int32 [4], replicated, may hold values from 1 to 2, as said below
- momenta: int32 [8, 8], replicated, may hold values from 0 to 7, as said below
Outputs:
- sigma: float32 [8, 64, 2, 128, 128], P('mom', ('sec', 'en'))
- polarization: float32 [4, 8, 3, 128], P('sec', 'mom')
Inputs may be any that keep to these rules, and one draw needn't show every extreme that they name: `offsets`: every mode's offset lies in 1 to 2; some mode's offset equals 2 and another mode's equals 1. momenta[k, k'] = p((k - k') mod 8) for a permutation p of the 8 phonon momenta.
All inputs are finite; a program needn't handle non-finite values.
Results may differ from a plain program's by a relative error of at most 0.014.
Values may be sent and summed in bfloat16 or wider, within the bound.
No kernel may reach another device: no remote copies, remote signals or barrier semaphores. Data moves between devices by JAX's collectives and lax.ppermute only.
A program may use at most 64 MiB of HBM per device.

v0:
```python
import math
import jax
import jax.numpy as jnp
from jax import lax
from jax.sharding import PartitionSpec as P


def passed_along(x, axis, by):
    peers = lax.axis_size(axis)
    pairs = [(i, i + by) for i in range(peers) if 0 <= i + by < peers]
    return lax.ppermute(x, axis, pairs)


def contract(former, latter):
    return jnp.sum(former[..., :, :, None, :] * latter[..., None, :, :, :], axis=-3)


def complex_product(former, latter):
    real_part = contract(former[..., 0, :, :, :], latter[..., 0, :, :, :]) - contract(
        former[..., 1, :, :, :], latter[..., 1, :, :, :]
    )
    imag_part = contract(former[..., 0, :, :, :], latter[..., 1, :, :, :]) + contract(
        former[..., 1, :, :, :], latter[..., 0, :, :, :]
    )
    return jnp.stack([real_part, imag_part], axis=-4)


def dyson_update(bare_phonon, prior_polar):
    return bare_phonon + complex_product(complex_product(bare_phonon, prior_polar), bare_phonon)


def flipped_products(blocks, derivative):
    flipped = jnp.einsum(
        "ktcbx,ixa->kticab", blocks, derivative, preferred_element_type=jnp.float32
    )
    sign_flip = jnp.array([1.0, -1.0], jnp.float32).reshape(1, 1, 1, 2, 1, 1)
    return (flipped * sign_flip).astype(jnp.bfloat16)


def mode_weights(chosen):
    real_part = chosen[:, :, 0]
    imag_part = chosen[:, :, 1]
    upper_part = jnp.stack([real_part, -imag_part], axis=2)
    lower_part = jnp.stack([imag_part, real_part], axis=2)
    return jnp.stack([upper_part, lower_part], axis=2)


def weighted_rows(weights, selected):
    mode_count = weights.shape[1]
    total = None
    for mode_index in range(mode_count):
        for part_index in range(2):
            for direction in range(3):
                factor = jnp.transpose(
                    weights[:, mode_index, :, part_index, direction, :, :], (0, 2, 1, 3)
                )
                slab = selected[direction, :, mode_index, part_index].astype(jnp.float32)
                term = factor[:, None, :, :, :, None] * slab[None, :, None, None, :, :]
                total = term if total is None else total + term
    return total.astype(jnp.bfloat16)


def point_terms(source, chosen, derivative, offsets, targets, levels, flipped):
    blocks = jnp.einsum(
        "iab,scbd->iscad", derivative, source, preferred_element_type=jnp.float32
    ).astype(jnp.bfloat16)
    mode_count = chosen.shape[1]
    selected = jnp.stack(
        [
            lax.dynamic_slice_in_dim(blocks, levels - offsets[mode_index], targets, 1)
            for mode_index in range(mode_count)
        ],
        axis=2,
    )
    weights = mode_weights(chosen)
    combined = weighted_rows(weights, selected)
    sigma_part = jnp.einsum(
        "ktjxab,jbd->ktxad", combined, derivative, preferred_element_type=jnp.float32
    )
    polar_part = jnp.einsum(
        "itmcab,kticab->kmia", selected, flipped, preferred_element_type=jnp.float32
    )
    return (sigma_part, polar_part)


def per_device(green_blocks, derivative, bare_phonon, prior_polar, offsets, momenta):
    points = green_blocks.shape[0]
    levels = green_blocks.shape[1]
    block_order = green_blocks.shape[-1]
    all_points = points * lax.axis_size("mom")
    all_levels = levels * lax.axis_size("sec") * lax.axis_size("en")
    phonon = dyson_update(bare_phonon, prior_polar)
    local_modes = phonon.shape[0]
    stacked = phonon.reshape((local_modes * points,) + phonon.shape[2:])
    gathered = lax.all_gather(stacked, ("sec", "mom"), axis=0, tiled=True)
    mode_count = gathered.shape[0] // all_points
    phonon_table = jnp.transpose(
        gathered.reshape((mode_count, all_points) + phonon.shape[2:]), (1, 0, 2, 3, 4, 5)
    )
    own_rows = lax.dynamic_slice_in_dim(momenta, lax.axis_index("mom") * points, points, 0)
    momentum_ids = lax.broadcasted_iota(jnp.int32, (points, all_points), 1)
    lower_rim = passed_along(green_blocks, ("sec", "en"), 1)
    travelling = jnp.concatenate([lower_rim, green_blocks], axis=1)
    targets = green_blocks.shape[1]
    flipped = flipped_products(green_blocks, derivative)
    initial = (
        jnp.zeros((points, targets, 2, block_order, block_order), jnp.float32),
        jnp.zeros((all_points, mode_count, 3, block_order), jnp.float32),
    )
    pieces = lax.all_gather(travelling, "mom", axis=0, tiled=True)

    def one_point(position, running):
        sigma_sum, polar_sum = running
        source = lax.dynamic_index_in_dim(pieces, position, 0, keepdims=False)
        column = lax.dynamic_index_in_dim(own_rows, position, 1, keepdims=False)
        onehot = (column[:, None] == momentum_ids).astype(jnp.float32)
        chosen = jnp.einsum(
            "kq,qmxija->kmxija", onehot, phonon_table, precision=lax.Precision.HIGHEST
        )
        sigma_part, polar_part = point_terms(
            source, chosen, derivative, offsets, targets, levels, flipped
        )
        polar_sum = polar_sum + jnp.einsum(
            "kq,kmia->qmia", onehot, polar_part, precision=lax.Precision.HIGHEST
        )
        return (sigma_sum + sigma_part, polar_sum)

    sigma_sum, polar_sum = lax.fori_loop(0, pieces.shape[0], one_point, initial)
    sigma_scale = 1.0 / math.sqrt(9.0 * mode_count * all_points)
    polar_scale = 1.0 / math.sqrt(float(all_points * all_levels * block_order))
    ordered = jnp.transpose(polar_sum, (1, 0, 2, 3))
    summed = lax.psum(ordered, ("sec", "mom", "en"))
    own_share = lax.dynamic_slice(
        summed,
        (lax.axis_index("sec") * local_modes, lax.axis_index("mom") * points, 0, 0),
        (local_modes, points, 3, block_order),
    )
    return (sigma_sum * sigma_scale, own_share * polar_scale)


def solution(mesh):
    return jax.shard_map(
        per_device,
        mesh=mesh,
        in_specs=(
            P("mom", ("sec", "en"), None, None, None),
            P(),
            P("sec", "mom", None, None, None, None),
            P("sec", "mom", None, None, None, None),
            P(),
            P(),
        ),
        out_specs=(P("mom", ("sec", "en"), None, None, None), P("sec", "mom", None, None)),
        check_vma=False,
    )
```

profile of v0, /device:TPU:1, one launch (start us, length us, event | category | flops | bytes accessed | tf_op | source)
XLA Modules:
  0.0 422.1 jit_solution(5566107944990981499)
XLA Ops:
  7.3 4.5 %collective-permute-start = (bf16[1,2,2,128,128]{4,3,2,1,0:T(8,128)(2,1)}, bf16[1,2,2,128,128]{4,3,2,1,0:T(8,128)(2,1)S(1)}, u32[]{:S(2)}, u32[]{:S(2)}) collective-permute-start(bf16[1,2,2,128,128]{4,3,2,1,0:T(8,128)(2,1)} %param.9), channel_id=1, source_target_pairs={{0,1},{1,2},{2,3},{3,4},{4,5},{5,6},{6,7},{7,64},{64,65},{65,66},{... | collective-permute-start | bytes 393224 | tf_op jit(solution)/shard_map/ppermute | solution.py:11
  11.8 7.9 %collective-permute-done = bf16[1,2,2,128,128]{4,3,2,1,0:T(8,128)(2,1)S(1)} collective-permute-done((bf16[1,2,2,128,128]{4,3,2,1,0:T(8,128)(2,1)}, bf16[1,2,2,128,128]{4,3,2,1,0:T(8,128)(2,1)S(1)}, u32[]{:S(2)}, u32[]{:S(2)}) %collective-permute-start) | collective-permute-done | bytes 131104 | tf_op jit(solution)/shard_map/ppermute | solution.py:11
  19.7 1.6 pad_maximum_fusion.1
  21.3 1.5 fusion.141
  30.5 69.0 %all-gather = f32[32,1,2,3,3,128]{5,2,4,3,1,0:T(2,128)S(1)} all-gather(f32[1,1,2,3,3,128]{5,2,4,3,1,0:T(2,128)S(1)} %copy.131), channel_id=2, replica_groups=mesh['sec'=4,'mom'=8,'en'=8] {'sec','mom'}, dimensions={0}, use_global_device_ids=true | all-gather | bytes 304128 | tf_op jit(solution)/shard_map/all_gather | solution.py:95
  100.7 235.9 %while.19 = (s32[]{:T(128)}, f32[1,2,2,128,128]{4,3,2,1,0:T(8,128)}, f32[8,4,3,128]{3,2,1,0:T(4,128)}, s32[1,8]{1,0:T(1,128)}, f32[8,4,2,3,3,128]{5,4,3,2,1,0:T(...) while((s32[]{:T(128)}, ...), condition=%wide.region_9.10_spmd.clone, body=%wide.region_8.9_spmd.clone.sunk | while | flops 167619600 | bytes 31974176 | solution.py:128
  100.7 1.3 constant_dynamic-slice_fusion.3
  105.8 1.4 convolution_convert_fusion.2
  123.1 6.8 %fusion.167 = f32[1,2,2,128,128]{4,3,2,1,0:T(8,128)} fusion(f32[2,128,128]{2,1,0:T(8,128)S(1)} %copy-done.12, f32[3,2,128]{2,0,1:T(4,128)S(1)} %get-tuple-element.669, f32[2,128,128]{2,1,0:T(8,128)S(1)} %copy-done.13, f32[3,2,128]{2,0,1:T(4,128)S(1)} %get-tuple-element.671, f32[2,128,128]{2,1,0:T(8,128)} %copy.209, ...), kind=kOutput, calls=%fused_computation.5.clone.1 | convolution fusion | flops 59899904 | bytes 3842049 | tf_op jit(solution)/shard_map/while/body/eval_jaxpr/ktjxab,jbd->ktxad/dot_general | solution.py:77
  129.9 1.3 constant_dynamic-slice_fusion.3
  135.0 1.4 convolution_convert_fusion.2
  152.4 7.1 %fusion.167 = f32[1,2,2,128,128]{4,3,2,1,0:T(8,128)} fusion(f32[2,128,128]{2,1,0:T(8,128)S(1)} %copy-done.12, f32[3,2,128]{2,0,1:T(4,128)S(1)} %get-tuple-element.669, f32[2,128,128]{2,1,0:T(8,128)S(1)} %copy-done.13, f32[3,2,128]{2,0,1:T(4,128)S(1)} %get-tuple-element.671, f32[2,128,128]{2,1,0:T(8,128)} %copy.209, ...), kind=kOutput, calls=%fused_computation.5.clone.1 | convolution fusion | flops 59899904 | bytes 3842049 | tf_op jit(solution)/shard_map/while/body/eval_jaxpr/ktjxab,jbd->ktxad/dot_general | solution.py:77
  159.4 1.3 constant_dynamic-slice_fusion.3
  164.5 1.4 convolution_convert_fusion.2
  181.9 7.1 %fusion.167 = f32[1,2,2,128,128]{4,3,2,1,0:T(8,128)} fusion(f32[2,128,128]{2,1,0:T(8,128)S(1)} %copy-done.12, f32[3,2,128]{2,0,1:T(4,128)S(1)} %get-tuple-element.669, f32[2,128,128]{2,1,0:T(8,128)S(1)} %copy-done.13, f32[3,2,128]{2,0,1:T(4,128)S(1)} %get-tuple-element.671, f32[2,128,128]{2,1,0:T(8,128)} %copy.209, ...), kind=kOutput, calls=%fused_computation.5.clone.1 | convolution fusion | flops 59899904 | bytes 3842049 | tf_op jit(solution)/shard_map/while/body/eval_jaxpr/ktjxab,jbd->ktxad/dot_general | solution.py:77
  189.0 1.3 constant_dynamic-slice_fusion.3
  194.1 1.3 convolution_convert_fusion.2
  211.4 7.1 %fusion.167 = f32[1,2,2,128,128]{4,3,2,1,0:T(8,128)} fusion(f32[2,128,128]{2,1,0:T(8,128)S(1)} %copy-done.12, f32[3,2,128]{2,0,1:T(4,128)S(1)} %get-tuple-element.669, f32[2,128,128]{2,1,0:T(8,128)S(1)} %copy-done.13, f32[3,2,128]{2,0,1:T(4,128)S(1)} %get-tuple-element.671, f32[2,128,128]{2,1,0:T(8,128)} %copy.209, ...), kind=kOutput, calls=%fused_computation.5.clone.1 | convolution fusion | flops 59899904 | bytes 3842049 | tf_op jit(solution)/shard_map/while/body/eval_jaxpr/ktjxab,jbd->ktxad/dot_general | solution.py:77
  218.5 1.3 constant_dynamic-slice_fusion.3
  223.6 1.4 convolution_convert_fusion.2
  240.9 7.1 %fusion.167 = f32[1,2,2,128,128]{4,3,2,1,0:T(8,128)} fusion(f32[2,128,128]{2,1,0:T(8,128)S(1)} %copy-done.12, f32[3,2,128]{2,0,1:T(4,128)S(1)} %get-tuple-element.669, f32[2,128,128]{2,1,0:T(8,128)S(1)} %copy-done.13, f32[3,2,128]{2,0,1:T(4,128)S(1)} %get-tuple-element.671, f32[2,128,128]{2,1,0:T(8,128)} %copy.209, ...), kind=kOutput, calls=%fused_computation.5.clone.1 | convolution fusion | flops 59899904 | bytes 3842049 | tf_op jit(solution)/shard_map/while/body/eval_jaxpr/ktjxab,jbd->ktxad/dot_general | solution.py:77
  248.0 1.3 constant_dynamic-slice_fusion.3
  253.1 1.4 convolution_convert_fusion.2
  270.5 7.1 %fusion.167 = f32[1,2,2,128,128]{4,3,2,1,0:T(8,128)} fusion(f32[2,128,128]{2,1,0:T(8,128)S(1)} %copy-done.12, f32[3,2,128]{2,0,1:T(4,128)S(1)} %get-tuple-element.669, f32[2,128,128]{2,1,0:T(8,128)S(1)} %copy-done.13, f32[3,2,128]{2,0,1:T(4,128)S(1)} %get-tuple-element.671, f32[2,128,128]{2,1,0:T(8,128)} %copy.209, ...), kind=kOutput, calls=%fused_computation.5.clone.1 | convolution fusion | flops 59899904 | bytes 3842049 | tf_op jit(solution)/shard_map/while/body/eval_jaxpr/ktjxab,jbd->ktxad/dot_general | solution.py:77
  277.5 1.3 constant_dynamic-slice_fusion.3
  282.6 1.4 convolution_convert_fusion.2
  300.0 7.1 %fusion.167 = f32[1,2,2,128,128]{4,3,2,1,0:T(8,128)} fusion(f32[2,128,128]{2,1,0:T(8,128)S(1)} %copy-done.12, f32[3,2,128]{2,0,1:T(4,128)S(1)} %get-tuple-element.669, f32[2,128,128]{2,1,0:T(8,128)S(1)} %copy-done.13, f32[3,2,128]{2,0,1:T(4,128)S(1)} %get-tuple-element.671, f32[2,128,128]{2,1,0:T(8,128)} %copy.209, ...), kind=kOutput, calls=%fused_computation.5.clone.1 | convolution fusion | flops 59899904 | bytes 3842049 | tf_op jit(solution)/shard_map/while/body/eval_jaxpr/ktjxab,jbd->ktxad/dot_general | solution.py:77
  307.1 1.3 constant_dynamic-slice_fusion.3
  312.1 1.4 convolution_convert_fusion.2
  329.5 7.1 %fusion.167 = f32[1,2,2,128,128]{4,3,2,1,0:T(8,128)} fusion(f32[2,128,128]{2,1,0:T(8,128)S(1)} %copy-done.12, f32[3,2,128]{2,0,1:T(4,128)S(1)} %get-tuple-element.669, f32[2,128,128]{2,1,0:T(8,128)S(1)} %copy-done.13, f32[3,2,128]{2,0,1:T(4,128)S(1)} %get-tuple-element.671, f32[2,128,128]{2,1,0:T(8,128)} %copy.209, ...), kind=kOutput, calls=%fused_computation.5.clone.1 | convolution fusion | flops 59899904 | bytes 3842049 | tf_op jit(solution)/shard_map/while/body/eval_jaxpr/ktjxab,jbd->ktxad/dot_general | solution.py:77
  337.4 75.5 %psum.7 = f32[4,8,3,128]{3,1,2,0:T(8,128)S(1)} all-reduce(f32[4,8,3,128]{3,1,2,0:T(8,128)S(1)} %bitcast.412), channel_id=1, replica_groups=mesh['sec'=4,'mom'=8,'en'=8] {'sec','mom','en'}, use_global_device_ids=true, to_apply=%region_10.11 | all-reduce | flops 12288 | bytes 98304 | tf_op jit(solution)/shard_map/psum | solution.py:132
  413.0 1.7 broadcast_multiply_fusion
  (592 shorter events, 160.6 us)
Async XLA Ops:
  7.2 92.9 %copy-start = (s32[8,8]{1,0:T(8,128)S(1)}, s32[8,8]{1,0:T(8,128)}, u32[]{:S(2)}) copy-start(s32[8,8]{1,0:T(8,128)} %param.14) | copy-start | bytes 772
  7.2 92.5 %copy-start.18 = (f32[2]{0:T(128)S(1)}, f32[2]{0:T(128)}, u32[]{:S(2)}) copy-start(f32[2]{0:T(128)} %constant.97.clone) | copy-start | bytes 28
  7.2 92.5 %copy-start.16 = (bf16[1,2,2,128,128]{4,3,2,1,0:T(8,128)(2,1)S(1)}, bf16[1,2,2,128,128]{4,3,2,1,0:T(8,128)(2,1)}, u32[]{:S(2)}) copy-start(bf16[1,2,2,128,128]{4,3,2,1,0:T(8,128)(2,1)} %param.9) | copy-start | bytes 393220
  7.2 92.5 %copy-start.1 = (bf16[3,128,128]{2,1,0:T(8,128)(2,1)S(1)}, bf16[3,128,128]{2,1,0:T(8,128)(2,1)}, u32[]{:S(2)}) copy-start(bf16[3,128,128]{2,1,0:T(8,128)(2,1)} %param.10) | copy-start | bytes 294916
  7.2 93.5 %all-gather.3.cloned.1.call-start = ((), (), s32[]{:S(2)}) async-start(), calls=%async_computation | async-start | bytes 2359296 | tf_op jit(solution)/shard_map/all_gather | solution.py:110
  7.3 12.4 %collective-permute-start = (bf16[1,2,2,128,128]{4,3,2,1,0:T(8,128)(2,1)}, bf16[1,2,2,128,128]{4,3,2,1,0:T(8,128)(2,1)S(1)}, u32[]{:S(2)}, u32[]{:S(2)}) collective-permute-start(bf16[1,2,2,128,128]{4,3,2,1,0:T(8,128)(2,1)} %param.9), channel_id=1, source_target_pairs={{0,1},{1,2},{2,3},{3,4},{4,5},{5,6},{6,7},{7,64},{64,65},{65,66},{... | collective-permute-start | bytes 393224 | tf_op jit(solution)/shard_map/ppermute | solution.py:11
  117.1 5.9 %copy-start.2 = (f32[2,128,128]{2,1,0:T(8,128)S(1)}, f32[2,128,128]{2,1,0:T(8,128)}, u32[]{:S(2)}) copy-start(f32[2,128,128]{2,1,0:T(8,128)} %copy.221) | copy-start | bytes 393220 | tf_op jit(solution)/shard_map/while
  117.2 5.9 %copy-start.3 = (f32[2,128,128]{2,1,0:T(8,128)S(1)}, f32[2,128,128]{2,1,0:T(8,128)}, u32[]{:S(2)}) copy-start(f32[2,128,128]{2,1,0:T(8,128)} %copy.222) | copy-start | bytes 393220 | tf_op jit(solution)/shard_map/while
  117.2 5.9 %copy-start.4 = (f32[2,128,128]{2,1,0:T(8,128)S(1)}, f32[2,128,128]{2,1,0:T(8,128)}, u32[]{:S(2)}) copy-start(f32[2,128,128]{2,1,0:T(8,128)} %copy.223) | copy-start | bytes 393220 | tf_op jit(solution)/shard_map/while
  117.2 5.9 %copy-start.5 = (f32[2,128,128]{2,1,0:T(8,128)S(1)}, f32[2,128,128]{2,1,0:T(8,128)}, u32[]{:S(2)}) copy-start(f32[2,128,128]{2,1,0:T(8,128)} %copy.224) | copy-start | bytes 393220 | tf_op jit(solution)/shard_map/while
  117.2 5.9 %copy-start.6 = (f32[2,128,128]{2,1,0:T(8,128)S(1)}, f32[2,128,128]{2,1,0:T(8,128)}, u32[]{:S(2)}) copy-start(f32[2,128,128]{2,1,0:T(8,128)} %copy.225) | copy-start | bytes 393220 | tf_op jit(solution)/shard_map/while
  117.2 5.9 %copy-start.7 = (f32[2,128,128]{2,1,0:T(8,128)S(1)}, f32[2,128,128]{2,1,0:T(8,128)}, u32[]{:S(2)}) copy-start(f32[2,128,128]{2,1,0:T(8,128)} %copy.226) | copy-start | bytes 393220 | tf_op jit(solution)/shard_map/while
  146.4 5.9 %copy-start.2 = (f32[2,128,128]{2,1,0:T(8,128)S(1)}, f32[2,128,128]{2,1,0:T(8,128)}, u32[]{:S(2)}) copy-start(f32[2,128,128]{2,1,0:T(8,128)} %copy.221) | copy-start | bytes 393220 | tf_op jit(solution)/shard_map/while
  146.4 5.9 %copy-start.3 = (f32[2,128,128]{2,1,0:T(8,128)S(1)}, f32[2,128,128]{2,1,0:T(8,128)}, u32[]{:S(2)}) copy-start(f32[2,128,128]{2,1,0:T(8,128)} %copy.222) | copy-start | bytes 393220 | tf_op jit(solution)/shard_map/while
  146.4 5.9 %copy-start.4 = (f32[2,128,128]{2,1,0:T(8,128)S(1)}, f32[2,128,128]{2,1,0:T(8,128)}, u32[]{:S(2)}) copy-start(f32[2,128,128]{2,1,0:T(8,128)} %copy.223) | copy-start | bytes 393220 | tf_op jit(solution)/shard_map/while
  146.4 5.9 %copy-start.5 = (f32[2,128,128]{2,1,0:T(8,128)S(1)}, f32[2,128,128]{2,1,0:T(8,128)}, u32[]{:S(2)}) copy-start(f32[2,128,128]{2,1,0:T(8,128)} %copy.224) | copy-start | bytes 393220 | tf_op jit(solution)/shard_map/while
  146.4 5.9 %copy-start.6 = (f32[2,128,128]{2,1,0:T(8,128)S(1)}, f32[2,128,128]{2,1,0:T(8,128)}, u32[]{:S(2)}) copy-start(f32[2,128,128]{2,1,0:T(8,128)} %copy.225) | copy-start | bytes 393220 | tf_op jit(solution)/shard_map/while
  146.4 5.9 %copy-start.7 = (f32[2,128,128]{2,1,0:T(8,128)S(1)}, f32[2,128,128]{2,1,0:T(8,128)}, u32[]{:S(2)}) copy-start(f32[2,128,128]{2,1,0:T(8,128)} %copy.226) | copy-start | bytes 393220 | tf_op jit(solution)/shard_map/while
  175.9 5.9 %copy-start.2 = (f32[2,128,128]{2,1,0:T(8,128)S(1)}, f32[2,128,128]{2,1,0:T(8,128)}, u32[]{:S(2)}) copy-start(f32[2,128,128]{2,1,0:T(8,128)} %copy.221) | copy-start | bytes 393220 | tf_op jit(solution)/shard_map/while
  175.9 5.9 %copy-start.3 = (f32[2,128,128]{2,1,0:T(8,128)S(1)}, f32[2,128,128]{2,1,0:T(8,128)}, u32[]{:S(2)}) copy-start(f32[2,128,128]{2,1,0:T(8,128)} %copy.222) | copy-start | bytes 393220 | tf_op jit(solution)/shard_map/while
  175.9 5.9 %copy-start.4 = (f32[2,128,128]{2,1,0:T(8,128)S(1)}, f32[2,128,128]{2,1,0:T(8,128)}, u32[]{:S(2)}) copy-start(f32[2,128,128]{2,1,0:T(8,128)} %copy.223) | copy-start | bytes 393220 | tf_op jit(solution)/shard_map/while
  175.9 5.9 %copy-start.5 = (f32[2,128,128]{2,1,0:T(8,128)S(1)}, f32[2,128,128]{2,1,0:T(8,128)}, u32[]{:S(2)}) copy-start(f32[2,128,128]{2,1,0:T(8,128)} %copy.224) | copy-start | bytes 393220 | tf_op jit(solution)/shard_map/while
  175.9 5.9 %copy-start.6 = (f32[2,128,128]{2,1,0:T(8,128)S(1)}, f32[2,128,128]{2,1,0:T(8,128)}, u32[]{:S(2)}) copy-start(f32[2,128,128]{2,1,0:T(8,128)} %copy.225) | copy-start | bytes 393220 | tf_op jit(solution)/shard_map/while
  176.0 5.9 %copy-start.7 = (f32[2,128,128]{2,1,0:T(8,128)S(1)}, f32[2,128,128]{2,1,0:T(8,128)}, u32[]{:S(2)}) copy-start(f32[2,128,128]{2,1,0:T(8,128)} %copy.226) | copy-start | bytes 393220 | tf_op jit(solution)/shard_map/while
  205.4 5.9 %copy-start.2 = (f32[2,128,128]{2,1,0:T(8,128)S(1)}, f32[2,128,128]{2,1,0:T(8,128)}, u32[]{:S(2)}) copy-start(f32[2,128,128]{2,1,0:T(8,128)} %copy.221) | copy-start | bytes 393220 | tf_op jit(solution)/shard_map/while
  205.4 5.9 %copy-start.3 = (f32[2,128,128]{2,1,0:T(8,128)S(1)}, f32[2,128,128]{2,1,0:T(8,128)}, u32[]{:S(2)}) copy-start(f32[2,128,128]{2,1,0:T(8,128)} %copy.222) | copy-start | bytes 393220 | tf_op jit(solution)/shard_map/while
  205.4 5.9 %copy-start.4 = (f32[2,128,128]{2,1,0:T(8,128)S(1)}, f32[2,128,128]{2,1,0:T(8,128)}, u32[]{:S(2)}) copy-start(f32[2,128,128]{2,1,0:T(8,128)} %copy.223) | copy-start | bytes 393220 | tf_op jit(solution)/shard_map/while
  205.5 5.9 %copy-start.5 = (f32[2,128,128]{2,1,0:T(8,128)S(1)}, f32[2,128,128]{2,1,0:T(8,128)}, u32[]{:S(2)}) copy-start(f32[2,128,128]{2,1,0:T(8,128)} %copy.224) | copy-start | bytes 393220 | tf_op jit(solution)/shard_map/while
  205.5 5.9 %copy-start.6 = (f32[2,128,128]{2,1,0:T(8,128)S(1)}, f32[2,128,128]{2,1,0:T(8,128)}, u32[]{:S(2)}) copy-start(f32[2,128,128]{2,1,0:T(8,128)} %copy.225) | copy-start | bytes 393220 | tf_op jit(solution)/shard_map/while
  205.5 5.9 %copy-start.7 = (f32[2,128,128]{2,1,0:T(8,128)S(1)}, f32[2,128,128]{2,1,0:T(8,128)}, u32[]{:S(2)}) copy-start(f32[2,128,128]{2,1,0:T(8,128)} %copy.226) | copy-start | bytes 393220 | tf_op jit(solution)/shard_map/while
  234.9 5.9 %copy-start.2 = (f32[2,128,128]{2,1,0:T(8,128)S(1)}, f32[2,128,128]{2,1,0:T(8,128)}, u32[]{:S(2)}) copy-start(f32[2,128,128]{2,1,0:T(8,128)} %copy.221) | copy-start | bytes 393220 | tf_op jit(solution)/shard_map/while
  235.0 5.9 %copy-start.3 = (f32[2,128,128]{2,1,0:T(8,128)S(1)}, f32[2,128,128]{2,1,0:T(8,128)}, u32[]{:S(2)}) copy-start(f32[2,128,128]{2,1,0:T(8,128)} %copy.222) | copy-start | bytes 393220 | tf_op jit(solution)/shard_map/while
  (94 other events, 303.5 us)
Sparse Core Ops, SparseCore 0:
  21.4 60.3 all-gather.2
where the time goes:
time: 428 us; the launch traced here: 422 us
  blocking collectives  145 us (34%)
  local copies, waits for them, and re-layouts  135 us (32%)
  matrix products  76.3 us (18%)
  other arithmetic  31.9 us (7%)
  between operations  19.4 us (5%)
  waiting for transfers between devices  7.91 us (2%)
  starting transfers between devices  4.53 us (1%)
    mul x192, local copies, waits for them, and re-layouts, weighted_rows(): term = factor[:, None, :, :, :, None] * slab[None, :, None, None, :, :]  108 us
    psum x1, blocking collectives, per_device(): summed = lax.psum(ordered, ('sec', 'mom', 'en'))  75.5 us
    all_gather x1, blocking collectives, per_device(): gathered = lax.all_gather(stacked, ('sec', 'mom'), axis=0, tiled=True)  69 us
    dot_general x8, matrix products, point_terms(): jnp.einsum('ktjxab,jbd->ktxad', combined, derivative, preferred_element_t...  56.2 us
    mul x40, other arithmetic, weighted_rows(): term = factor[:, None, :, :, :, None] * slab[None, :, None, None, :, :]  12.7 us
    dot_general x8, matrix products, point_terms(): jnp.einsum('iab,scbd->iscad', derivative, source, preferred_element_type=...  10.8 us
    dynamic_slice x8, local copies, waits for them, and re-layouts, one_point(): column = lax.dynamic_index_in_dim(own_rows, position, 1, keepdims=False)  10.7 us
    another operation x8, other arithmetic  10.2 us
  transfers between devices with their start and end apart: 2, of which 1 were waited for; matrix products, arithmetic and copies ran while one was open for 1% of the time, Pallas kernels for 0%

commit v1 on v0

--- a/solution.py
+++ b/solution.py
@@ -92,7 +92,10 @@
     phonon = dyson_update(bare_phonon, prior_polar)
     local_modes = phonon.shape[0]
     stacked = phonon.reshape((local_modes * points,) + phonon.shape[2:])
-    gathered = lax.all_gather(stacked, ("sec", "mom"), axis=0, tiled=True)
+    gathered = jnp.concatenate(
+        lax.all_to_all(jnp.stack([stacked] * lax.axis_size(("sec", "mom"))), ("sec", "mom"), 0, 0),
+        axis=0,
+    )
     mode_count = gathered.shape[0] // all_points
     phonon_table = jnp.transpose(
         gathered.reshape((mode_count, all_points) + phonon.shape[2:]), (1, 0, 2, 3, 4, 5)

time: 428 us -> 406 us (0.949)
  blocking collectives: 145 us -> 77.3 us
  waiting for transfers between devices: 7.91 us -> 49.3 us
  starting transfers between devices: 4.53 us -> 11.7 us
    all_gather x1 -> x0, blocking collectives: 69 us -> none  [per_device(): gathered = lax.all_gather(stacked, ('sec', 'mom'), axis=0, tiled=True)]
    all_gather x1, waiting for transfers between devices: 0.01 us -> 37.5 us  [per_device(): pieces = lax.all_gather(travelling, 'mom', axis=0, tiled=True)]
    all_to_all x0 -> x1, starting transfers between devices: none -> 7.2 us  [per_device(): lax.all_to_all(jnp.stack([stacked] * lax.axis_size(('sec', 'mom'))), ('se...]
  transfers between devices with their start and end apart: 2 -> 3, of which waited for: 1 -> 3; matrix products, arithmetic and copies ran while one was open for 1% -> 1% of each run, Pallas kernels for 0% -> 0%
where the time goes in v1:
time: 406 us; the launch traced here: 400 us
  local copies, waits for them, and re-layouts  133 us (33%)
  blocking collectives  77.3 us (19%)
  matrix products  75.7 us (19%)
  waiting for transfers between devices  49.3 us (12%)
  other arithmetic  31.2 us (8%)
  between operations  19.4 us (5%)
  starting transfers between devices  11.7 us (3%)
    mul x192, local copies, waits for them, and re-layouts, weighted_rows(): term = factor[:, None, :, :, :, None] * slab[None, :, None, None, :, :]  107 us
    psum x1, blocking collectives, per_device(): summed = lax.psum(ordered, ('sec', 'mom', 'en'))  77.3 us
    dot_general x8, matrix products, point_terms(): jnp.einsum('ktjxab,jbd->ktxad', combined, derivative, preferred_element_t...  56.2 us
    all_gather x1, waiting for transfers between devices, per_device(): pieces = lax.all_gather(travelling, 'mom', axis=0, tiled=True)  37.5 us
    mul x40, other arithmetic, weighted_rows(): term = factor[:, None, :, :, :, None] * slab[None, :, None, None, :, :]  12.8 us
    dot_general x8, matrix products, point_terms(): jnp.einsum('iab,scbd->iscad', derivative, source, preferred_element_type=...  10.8 us
    dynamic_slice x8, local copies, waits for them, and re-layouts, one_point(): column = lax.dynamic_index_in_dim(own_rows, position, 1, keepdims=False)  10 us
    while x256, local copies, waits for them, and re-layouts  9.92 us
  transfers between devices with their start and end apart: 3, of which 3 were waited for; matrix products, arithmetic and copies ran while one was open for 1% of the time, Pallas kernels for 0%

profile of v1, /device:TPU:1, one launch (start us, length us, event | category | flops | bytes accessed | tf_op | source)
XLA Modules:
  0.0 400.3 jit_solution(10660584739055606494)
XLA Ops:
  7.3 4.5 %collective-permute-start = (bf16[1,2,2,128,128]{4,3,2,1,0:T(8,128)(2,1)}, bf16[1,2,2,128,128]{4,3,2,1,0:T(8,128)(2,1)S(1)}, u32[]{:S(2)}, u32[]{:S(2)}) collective-permute-start(bf16[1,2,2,128,128]{4,3,2,1,0:T(8,128)(2,1)} %param.9), channel_id=1, source_target_pairs={{0,1},{1,2},{2,3},{3,4},{4,5},{5,6},{6,7},{7,64},{64,65},{65,66},{... | collective-permute-start | bytes 393224 | tf_op jit(solution)/shard_map/ppermute | solution.py:11
  11.8 7.9 %collective-permute-done = bf16[1,2,2,128,128]{4,3,2,1,0:T(8,128)(2,1)S(1)} collective-permute-done((bf16[1,2,2,128,128]{4,3,2,1,0:T(8,128)(2,1)}, bf16[1,2,2,128,128]{4,3,2,1,0:T(8,128)(2,1)S(1)}, u32[]{:S(2)}, u32[]{:S(2)}) %collective-permute-start) | collective-permute-done | bytes 131104 | tf_op jit(solution)/shard_map/ppermute | solution.py:11
  19.7 1.6 pad_maximum_fusion.1
  24.7 7.2 %all-to-all-start = ((f32[32,1,2,3,3,128]{5,2,4,3,1,0:T(2,128)}), f32[32,1,2,3,3,128]{5,2,4,3,1,0:T(2,128)S(1)}, u32[]{:S(2)}, u32[]{:S(2)}) async-start(f32[32,1,2,3,3,128]{5,2,4,3,1,0:T(2,128)} %stack.112), calls=%async_computation | async-start | bytes 589824 | tf_op jit(solution)/shard_map/all_to_all | solution.py:96
  38.6 3.9 all-to-all-done
  42.8 37.5 %all-gather.2.cloned.1.call-done = bf16[8,4,2,128,128]{4,3,2,1,0:T(8,128)(2,1)} async-done(((bf16[1,4,2,128,128]{4,3,2,1,0:T(8,128)(2,1)}), bf16[8,4,2,128,128]{4,3,2,1,0:T(8,128)(2,1)}) %all-gather.2.cloned.1.call-update) | async-done | bytes 2097168 | tf_op jit(solution)/shard_map/all_gather | solution.py:113
  80.3 232.8 %while.19 = (s32[]{:T(128)}, f32[1,2,2,128,128]{4,3,2,1,0:T(8,128)}, f32[8,4,3,128]{3,2,1,0:T(4,128)}, s32[1,8]{1,0:T(1,128)}, f32[8,4,2,3,3,128]{5,4,3,2,1,0:T(...) while((s32[]{:T(128)}, ...), condition=%wide.region_9.10_spmd.clone, body=%wide.region_8.9_spmd.clone.sunk | while | flops 167619600 | bytes 31974176 | solution.py:131
  85.1 1.3 convolution_convert_fusion.2
  102.3 6.8 %fusion.168 = f32[1,2,2,128,128]{4,3,2,1,0:T(8,128)} fusion(f32[2,128,128]{2,1,0:T(8,128)S(1)} %copy-done.12, f32[3,2,128]{2,0,1:T(4,128)S(1)} %get-tuple-element.681, f32[2,128,128]{2,1,0:T(8,128)S(1)} %copy-done.13, f32[3,2,128]{2,0,1:T(4,128)S(1)} %get-tuple-element.683, f32[2,128,128]{2,1,0:T(8,128)} %copy.241, ...), kind=kOutput, calls=%fused_computation.5.clone.1 | convolution fusion | flops 59899904 | bytes 3842049 | tf_op jit(solution)/shard_map/while/body/eval_jaxpr/ktjxab,jbd->ktxad/dot_general | solution.py:77
  109.1 1.3 constant_dynamic-slice_fusion.3
  114.0 1.3 convolution_convert_fusion.2
  131.2 7.1 %fusion.168 = f32[1,2,2,128,128]{4,3,2,1,0:T(8,128)} fusion(f32[2,128,128]{2,1,0:T(8,128)S(1)} %copy-done.12, f32[3,2,128]{2,0,1:T(4,128)S(1)} %get-tuple-element.681, f32[2,128,128]{2,1,0:T(8,128)S(1)} %copy-done.13, f32[3,2,128]{2,0,1:T(4,128)S(1)} %get-tuple-element.683, f32[2,128,128]{2,1,0:T(8,128)} %copy.241, ...), kind=kOutput, calls=%fused_computation.5.clone.1 | convolution fusion | flops 59899904 | bytes 3842049 | tf_op jit(solution)/shard_map/while/body/eval_jaxpr/ktjxab,jbd->ktxad/dot_general | solution.py:77
  138.3 1.3 constant_dynamic-slice_fusion.3
  143.1 1.3 convolution_convert_fusion.2
  160.3 7.1 %fusion.168 = f32[1,2,2,128,128]{4,3,2,1,0:T(8,128)} fusion(f32[2,128,128]{2,1,0:T(8,128)S(1)} %copy-done.12, f32[3,2,128]{2,0,1:T(4,128)S(1)} %get-tuple-element.681, f32[2,128,128]{2,1,0:T(8,128)S(1)} %copy-done.13, f32[3,2,128]{2,0,1:T(4,128)S(1)} %get-tuple-element.683, f32[2,128,128]{2,1,0:T(8,128)} %copy.241, ...), kind=kOutput, calls=%fused_computation.5.clone.1 | convolution fusion | flops 59899904 | bytes 3842049 | tf_op jit(solution)/shard_map/while/body/eval_jaxpr/ktjxab,jbd->ktxad/dot_general | solution.py:77
  167.4 1.3 constant_dynamic-slice_fusion.3
  172.3 1.3 convolution_convert_fusion.2
  189.5 7.1 %fusion.168 = f32[1,2,2,128,128]{4,3,2,1,0:T(8,128)} fusion(f32[2,128,128]{2,1,0:T(8,128)S(1)} %copy-done.12, f32[3,2,128]{2,0,1:T(4,128)S(1)} %get-tuple-element.681, f32[2,128,128]{2,1,0:T(8,128)S(1)} %copy-done.13, f32[3,2,128]{2,0,1:T(4,128)S(1)} %get-tuple-element.683, f32[2,128,128]{2,1,0:T(8,128)} %copy.241, ...), kind=kOutput, calls=%fused_computation.5.clone.1 | convolution fusion | flops 59899904 | bytes 3842049 | tf_op jit(solution)/shard_map/while/body/eval_jaxpr/ktjxab,jbd->ktxad/dot_general | solution.py:77
  196.6 1.3 constant_dynamic-slice_fusion.3
  201.4 1.4 convolution_convert_fusion.2
  218.6 7.1 %fusion.168 = f32[1,2,2,128,128]{4,3,2,1,0:T(8,128)} fusion(f32[2,128,128]{2,1,0:T(8,128)S(1)} %copy-done.12, f32[3,2,128]{2,0,1:T(4,128)S(1)} %get-tuple-element.681, f32[2,128,128]{2,1,0:T(8,128)S(1)} %copy-done.13, f32[3,2,128]{2,0,1:T(4,128)S(1)} %get-tuple-element.683, f32[2,128,128]{2,1,0:T(8,128)} %copy.241, ...), kind=kOutput, calls=%fused_computation.5.clone.1 | convolution fusion | flops 59899904 | bytes 3842049 | tf_op jit(solution)/shard_map/while/body/eval_jaxpr/ktjxab,jbd->ktxad/dot_general | solution.py:77
  225.7 1.3 constant_dynamic-slice_fusion.3
  230.5 1.3 convolution_convert_fusion.2
  247.8 7.1 %fusion.168 = f32[1,2,2,128,128]{4,3,2,1,0:T(8,128)} fusion(f32[2,128,128]{2,1,0:T(8,128)S(1)} %copy-done.12, f32[3,2,128]{2,0,1:T(4,128)S(1)} %get-tuple-element.681, f32[2,128,128]{2,1,0:T(8,128)S(1)} %copy-done.13, f32[3,2,128]{2,0,1:T(4,128)S(1)} %get-tuple-element.683, f32[2,128,128]{2,1,0:T(8,128)} %copy.241, ...), kind=kOutput, calls=%fused_computation.5.clone.1 | convolution fusion | flops 59899904 | bytes 3842049 | tf_op jit(solution)/shard_map/while/body/eval_jaxpr/ktjxab,jbd->ktxad/dot_general | solution.py:77
  254.8 1.3 constant_dynamic-slice_fusion.3
  259.7 1.3 convolution_convert_fusion.2
  276.9 7.1 %fusion.168 = f32[1,2,2,128,128]{4,3,2,1,0:T(8,128)} fusion(f32[2,128,128]{2,1,0:T(8,128)S(1)} %copy-done.12, f32[3,2,128]{2,0,1:T(4,128)S(1)} %get-tuple-element.681, f32[2,128,128]{2,1,0:T(8,128)S(1)} %copy-done.13, f32[3,2,128]{2,0,1:T(4,128)S(1)} %get-tuple-element.683, f32[2,128,128]{2,1,0:T(8,128)} %copy.241, ...), kind=kOutput, calls=%fused_computation.5.clone.1 | convolution fusion | flops 59899904 | bytes 3842049 | tf_op jit(solution)/shard_map/while/body/eval_jaxpr/ktjxab,jbd->ktxad/dot_general | solution.py:77
  284.0 1.3 constant_dynamic-slice_fusion.3
  288.8 1.4 convolution_convert_fusion.2
  306.0 7.1 %fusion.168 = f32[1,2,2,128,128]{4,3,2,1,0:T(8,128)} fusion(f32[2,128,128]{2,1,0:T(8,128)S(1)} %copy-done.12, f32[3,2,128]{2,0,1:T(4,128)S(1)} %get-tuple-element.681, f32[2,128,128]{2,1,0:T(8,128)S(1)} %copy-done.13, f32[3,2,128]{2,0,1:T(4,128)S(1)} %get-tuple-element.683, f32[2,128,128]{2,1,0:T(8,128)} %copy.241, ...), kind=kOutput, calls=%fused_computation.5.clone.1 | convolution fusion | flops 59899904 | bytes 3842049 | tf_op jit(solution)/shard_map/while/body/eval_jaxpr/ktjxab,jbd->ktxad/dot_general | solution.py:77
  314.0 77.3 %psum.7 = f32[4,8,3,128]{3,1,2,0:T(8,128)S(1)} all-reduce(f32[4,8,3,128]{3,1,2,0:T(8,128)S(1)} %bitcast.414), channel_id=1, replica_groups=mesh['sec'=4,'mom'=8,'en'=8] {'sec','mom','en'}, use_global_device_ids=true, to_apply=%region_10.11 | all-reduce | flops 12288 | bytes 98304 | tf_op jit(solution)/shard_map/psum | solution.py:135
  391.3 1.7 broadcast_multiply_fusion
  (596 shorter events, 160.8 us)
Async XLA Ops:
  7.2 30.9 %copy-start = (s32[8,8]{1,0:T(8,128)S(1)}, s32[8,8]{1,0:T(8,128)}, u32[]{:S(2)}) copy-start(s32[8,8]{1,0:T(8,128)} %param.14) | copy-start | bytes 772
  7.2 30.5 %copy-start.19 = (f32[2]{0:T(128)S(1)}, f32[2]{0:T(128)}, u32[]{:S(2)}) copy-start(f32[2]{0:T(128)} %constant.97.clone) | copy-start | bytes 28
  7.2 30.5 %copy-start.16 = (bf16[1,2,2,128,128]{4,3,2,1,0:T(8,128)(2,1)S(1)}, bf16[1,2,2,128,128]{4,3,2,1,0:T(8,128)(2,1)}, u32[]{:S(2)}) copy-start(bf16[1,2,2,128,128]{4,3,2,1,0:T(8,128)(2,1)} %param.9) | copy-start | bytes 393220
  7.2 24.7 %copy-start.18 = (s32[4]{0:T(128)S(1)}, s32[4]{0:T(128)}, u32[]{:S(2)}) copy-start(s32[4]{0:T(128)} %param.13) | copy-start | bytes 52
  7.2 30.5 %copy-start.1 = (bf16[3,128,128]{2,1,0:T(8,128)(2,1)S(1)}, bf16[3,128,128]{2,1,0:T(8,128)(2,1)}, u32[]{:S(2)}) copy-start(bf16[3,128,128]{2,1,0:T(8,128)(2,1)} %param.10) | copy-start | bytes 294916
  7.2 73.1 %all-gather.2.cloned.1.call-start = ((), (), s32[]{:S(2)}) async-start(), calls=%async_computation.1 | async-start | bytes 2359296 | tf_op jit(solution)/shard_map/all_gather | solution.py:113
  7.3 12.4 %collective-permute-start = (bf16[1,2,2,128,128]{4,3,2,1,0:T(8,128)(2,1)}, bf16[1,2,2,128,128]{4,3,2,1,0:T(8,128)(2,1)S(1)}, u32[]{:S(2)}, u32[]{:S(2)}) collective-permute-start(bf16[1,2,2,128,128]{4,3,2,1,0:T(8,128)(2,1)} %param.9), channel_id=1, source_target_pairs={{0,1},{1,2},{2,3},{3,4},{4,5},{5,6},{6,7},{7,64},{64,65},{65,66},{... | collective-permute-start | bytes 393224 | tf_op jit(solution)/shard_map/ppermute | solution.py:11
  24.7 17.9 %all-to-all-start = ((f32[32,1,2,3,3,128]{5,2,4,3,1,0:T(2,128)}), f32[32,1,2,3,3,128]{5,2,4,3,1,0:T(2,128)S(1)}, u32[]{:S(2)}, u32[]{:S(2)}) async-start(f32[32,1,2,3,3,128]{5,2,4,3,1,0:T(2,128)} %stack.112), calls=%async_computation | async-start | bytes 589824 | tf_op jit(solution)/shard_map/all_to_all | solution.py:96
  96.4 5.8 %copy-start.2 = (f32[2,128,128]{2,1,0:T(8,128)S(1)}, f32[2,128,128]{2,1,0:T(8,128)}, u32[]{:S(2)}) copy-start(f32[2,128,128]{2,1,0:T(8,128)} %copy.253) | copy-start | bytes 393220 | tf_op jit(solution)/shard_map/while
  96.4 5.8 %copy-start.3 = (f32[2,128,128]{2,1,0:T(8,128)S(1)}, f32[2,128,128]{2,1,0:T(8,128)}, u32[]{:S(2)}) copy-start(f32[2,128,128]{2,1,0:T(8,128)} %copy.254) | copy-start | bytes 393220 | tf_op jit(solution)/shard_map/while
  96.4 5.8 %copy-start.4 = (f32[2,128,128]{2,1,0:T(8,128)S(1)}, f32[2,128,128]{2,1,0:T(8,128)}, u32[]{:S(2)}) copy-start(f32[2,128,128]{2,1,0:T(8,128)} %copy.255) | copy-start | bytes 393220 | tf_op jit(solution)/shard_map/while
  96.4 5.8 %copy-start.5 = (f32[2,128,128]{2,1,0:T(8,128)S(1)}, f32[2,128,128]{2,1,0:T(8,128)}, u32[]{:S(2)}) copy-start(f32[2,128,128]{2,1,0:T(8,128)} %copy.256) | copy-start | bytes 393220 | tf_op jit(solution)/shard_map/while
  96.5 5.8 %copy-start.6 = (f32[2,128,128]{2,1,0:T(8,128)S(1)}, f32[2,128,128]{2,1,0:T(8,128)}, u32[]{:S(2)}) copy-start(f32[2,128,128]{2,1,0:T(8,128)} %copy.257) | copy-start | bytes 393220 | tf_op jit(solution)/shard_map/while
  96.5 5.8 %copy-start.7 = (f32[2,128,128]{2,1,0:T(8,128)S(1)}, f32[2,128,128]{2,1,0:T(8,128)}, u32[]{:S(2)}) copy-start(f32[2,128,128]{2,1,0:T(8,128)} %copy.258) | copy-start | bytes 393220 | tf_op jit(solution)/shard_map/while
  125.3 5.8 %copy-start.2 = (f32[2,128,128]{2,1,0:T(8,128)S(1)}, f32[2,128,128]{2,1,0:T(8,128)}, u32[]{:S(2)}) copy-start(f32[2,128,128]{2,1,0:T(8,128)} %copy.253) | copy-start | bytes 393220 | tf_op jit(solution)/shard_map/while
  125.3 5.8 %copy-start.3 = (f32[2,128,128]{2,1,0:T(8,128)S(1)}, f32[2,128,128]{2,1,0:T(8,128)}, u32[]{:S(2)}) copy-start(f32[2,128,128]{2,1,0:T(8,128)} %copy.254) | copy-start | bytes 393220 | tf_op jit(solution)/shard_map/while
  125.3 5.8 %copy-start.4 = (f32[2,128,128]{2,1,0:T(8,128)S(1)}, f32[2,128,128]{2,1,0:T(8,128)}, u32[]{:S(2)}) copy-start(f32[2,128,128]{2,1,0:T(8,128)} %copy.255) | copy-start | bytes 393220 | tf_op jit(solution)/shard_map/while
  125.3 5.8 %copy-start.5 = (f32[2,128,128]{2,1,0:T(8,128)S(1)}, f32[2,128,128]{2,1,0:T(8,128)}, u32[]{:S(2)}) copy-start(f32[2,128,128]{2,1,0:T(8,128)} %copy.256) | copy-start | bytes 393220 | tf_op jit(solution)/shard_map/while
  125.3 5.8 %copy-start.6 = (f32[2,128,128]{2,1,0:T(8,128)S(1)}, f32[2,128,128]{2,1,0:T(8,128)}, u32[]{:S(2)}) copy-start(f32[2,128,128]{2,1,0:T(8,128)} %copy.257) | copy-start | bytes 393220 | tf_op jit(solution)/shard_map/while
  125.3 5.8 %copy-start.7 = (f32[2,128,128]{2,1,0:T(8,128)S(1)}, f32[2,128,128]{2,1,0:T(8,128)}, u32[]{:S(2)}) copy-start(f32[2,128,128]{2,1,0:T(8,128)} %copy.258) | copy-start | bytes 393220 | tf_op jit(solution)/shard_map/while
  154.4 5.8 %copy-start.2 = (f32[2,128,128]{2,1,0:T(8,128)S(1)}, f32[2,128,128]{2,1,0:T(8,128)}, u32[]{:S(2)}) copy-start(f32[2,128,128]{2,1,0:T(8,128)} %copy.253) | copy-start | bytes 393220 | tf_op jit(solution)/shard_map/while
  154.4 5.8 %copy-start.3 = (f32[2,128,128]{2,1,0:T(8,128)S(1)}, f32[2,128,128]{2,1,0:T(8,128)}, u32[]{:S(2)}) copy-start(f32[2,128,128]{2,1,0:T(8,128)} %copy.254) | copy-start | bytes 393220 | tf_op jit(solution)/shard_map/while
  154.4 5.8 %copy-start.4 = (f32[2,128,128]{2,1,0:T(8,128)S(1)}, f32[2,128,128]{2,1,0:T(8,128)}, u32[]{:S(2)}) copy-start(f32[2,128,128]{2,1,0:T(8,128)} %copy.255) | copy-start | bytes 393220 | tf_op jit(solution)/shard_map/while
  154.4 5.8 %copy-start.5 = (f32[2,128,128]{2,1,0:T(8,128)S(1)}, f32[2,128,128]{2,1,0:T(8,128)}, u32[]{:S(2)}) copy-start(f32[2,128,128]{2,1,0:T(8,128)} %copy.256) | copy-start | bytes 393220 | tf_op jit(solution)/shard_map/while
  154.4 5.8 %copy-start.6 = (f32[2,128,128]{2,1,0:T(8,128)S(1)}, f32[2,128,128]{2,1,0:T(8,128)}, u32[]{:S(2)}) copy-start(f32[2,128,128]{2,1,0:T(8,128)} %copy.257) | copy-start | bytes 393220 | tf_op jit(solution)/shard_map/while
  154.5 5.8 %copy-start.7 = (f32[2,128,128]{2,1,0:T(8,128)S(1)}, f32[2,128,128]{2,1,0:T(8,128)}, u32[]{:S(2)}) copy-start(f32[2,128,128]{2,1,0:T(8,128)} %copy.258) | copy-start | bytes 393220 | tf_op jit(solution)/shard_map/while
  183.5 5.8 %copy-start.2 = (f32[2,128,128]{2,1,0:T(8,128)S(1)}, f32[2,128,128]{2,1,0:T(8,128)}, u32[]{:S(2)}) copy-start(f32[2,128,128]{2,1,0:T(8,128)} %copy.253) | copy-start | bytes 393220 | tf_op jit(solution)/shard_map/while
  183.6 5.8 %copy-start.3 = (f32[2,128,128]{2,1,0:T(8,128)S(1)}, f32[2,128,128]{2,1,0:T(8,128)}, u32[]{:S(2)}) copy-start(f32[2,128,128]{2,1,0:T(8,128)} %copy.254) | copy-start | bytes 393220 | tf_op jit(solution)/shard_map/while
  183.6 5.8 %copy-start.4 = (f32[2,128,128]{2,1,0:T(8,128)S(1)}, f32[2,128,128]{2,1,0:T(8,128)}, u32[]{:S(2)}) copy-start(f32[2,128,128]{2,1,0:T(8,128)} %copy.255) | copy-start | bytes 393220 | tf_op jit(solution)/shard_map/while
  183.6 5.8 %copy-start.5 = (f32[2,128,128]{2,1,0:T(8,128)S(1)}, f32[2,128,128]{2,1,0:T(8,128)}, u32[]{:S(2)}) copy-start(f32[2,128,128]{2,1,0:T(8,128)} %copy.256) | copy-start | bytes 393220 | tf_op jit(solution)/shard_map/while
  183.6 5.8 %copy-start.6 = (f32[2,128,128]{2,1,0:T(8,128)S(1)}, f32[2,128,128]{2,1,0:T(8,128)}, u32[]{:S(2)}) copy-start(f32[2,128,128]{2,1,0:T(8,128)} %copy.257) | copy-start | bytes 393220 | tf_op jit(solution)/shard_map/while
  183.6 5.8 %copy-start.7 = (f32[2,128,128]{2,1,0:T(8,128)S(1)}, f32[2,128,128]{2,1,0:T(8,128)}, u32[]{:S(2)}) copy-start(f32[2,128,128]{2,1,0:T(8,128)} %copy.258) | copy-start | bytes 393220 | tf_op jit(solution)/shard_map/while
  (96 other events, 311.8 us)
Sparse Core Ops, SparseCore 0:
  21.4 58.7 all-gather.1
